TPU v7x, 32 devices: a whole 2x2x4 slice. The times are simulated.
32 devices in a mesh: dp: 4 (over y, x), seqtp: 8 (over z, core).
Axes of the slice: x: 2, y: 2, z: 4, core: 2. Of those that a mesh axis runs over, the one named last changes fastest.
Arguments:
- output_gradient: bfloat16 [2048, 4096], P(('dp', 'seqtp')), may hold values from -6 to 6
- hidden: bfloat16 [2048, 14336], P('dp', 'seqtp'), may hold values from -6 to 6
- frozen_down_weight: bfloat16 [14336, 4096], P('seqtp'), may hold values from -0.09375 to 0.09375
- adapter_input_maps: bfloat16 [24, 16, 14336], P('dp', None, 'seqtp'), may hold values from -0.1875 to 0.1875
- adapter_output_maps: bfloat16 [24, 16, 4096], P('dp', None, 'seqtp'), may hold values from -0.09375 to 0.09375
- adapter_per_block: int32 [4, 4], replicated, may hold values from 0 to 23
- live_tokens_per_block: int32 [4, 4], replicated, may hold values from 1 to 128, as said below
Outputs:
- hidden_gradient: bfloat16 [2048, 14336], P('dp', 'seqtp')
- adapter_input_gradient: float32 [24, 16, 14336], P('dp', None, 'seqtp')
- adapter_output_gradient: float32 [24, 16, 4096], P('dp', None, 'seqtp')
Inputs may be any that keep to these rules, and one draw needn't show every extreme that they name: The first live_tokens_per_block tokens of a block are live, the rest padding; some block is full.
All inputs are finite; a program needn't handle non-finite values.
Results may differ from a plain program's by a relative error of at most 0.0034.
Values may be sent and summed in bfloat16 or wider, within the bound.
A program may use at most 64 MiB of HBM per device.

v0:
```python
import functools

import jax
import jax.numpy as jnp
from jax import lax
from jax.experimental import pallas as pl
from jax.experimental.pallas import tpu as pltpu
from jax.sharding import PartitionSpec as P

adapter_scale = 0.5
MESH = pl.DeviceIdType.MESH
F32 = jnp.float32
BF16 = jnp.bfloat16


def dot_nt(a, b):
    return lax.dot_general(a, b, (((1,), (1,)), ((), ())), preferred_element_type=F32)


def dot_nn(a, b):
    return lax.dot_general(a, b, (((1,), (0,)), ((), ())), preferred_element_type=F32)


def kernel(
    nd, ntp, blocks, block, rank, held, rows, chunks, ff, feat, tiles,
    g_ref, h_ref, w_ref, a_ref, b_ref, tab, live,
    hg_ref, oa_ref, ob_ref,
    g_all, h_v, w_v, a_all, b_all, a_sel, b_sel, b_in, lo_all, lo_bf, lo_t,
    li_part, li_rs, li_all, li_bf, ga, gb, acc, hg_v, oa_v, ob_v,
    w_sem, own_sem, out_sem,
    nb_s, nb_r, sib_s, sib_r, bdp_s, bdp_r, adp_s, adp_r, bs_s, bs_r,
    lo_s, lo_r, rs_s, rs_r, li_s, li_r, ga_s, ga_r, gb_s, gb_r,
):
    nz = ntp // 2
    dp = lax.axis_index("dp")
    j = lax.axis_index("seqtp")
    z = lax.div(j, 2)
    c = lax.rem(j, 2)
    sib = z * 2 + 1 - c
    crow = rows // chunks
    tile = ff // tiles
    pair = 2 * rows
    piece = blocks * rank // ntp
    fused = pair == block

    def dp_peer(k):
        return lax.rem(dp + k, nd)

    def tp_peer(k):
        return lax.rem(j + k, ntp)

    def dp_from(k):
        return lax.rem(dp + nd - k, nd)

    def tp_from(k):
        return lax.rem(j + ntp - k, ntp)

    def slab(index, size):
        return pl.ds(pl.multiple_of(index * size, size), size)

    w_cp = lambda n: pltpu.make_async_copy(
        w_ref.at[slab(n, tile)], w_v.at[slab(n, tile)], w_sem.at[n]
    )
    own = [
        pltpu.make_async_copy(g_ref, g_all.at[slab(j, rows)], own_sem.at[0]),
        pltpu.make_async_copy(b_ref, b_all.at[pl.ds(dp * held, held)], own_sem.at[1]),
        pltpu.make_async_copy(h_ref, h_v, own_sem.at[2]),
        pltpu.make_async_copy(a_ref, a_all.at[pl.ds(dp * held, held)], own_sem.at[3]),
    ]
    own[0].start()
    own[1].start()
    for n in range(tiles):
        w_cp(n).start()
    own[2].start()
    own[3].start()

    barrier = pltpu.get_barrier_semaphore()
    for k in range(1, nd):
        pl.semaphore_signal(barrier, inc=1, device_id=(dp_peer(k), j), device_id_type=MESH)
    for k in range(1, ntp):
        pl.semaphore_signal(barrier, inc=1, device_id=(dp, tp_peer(k)), device_id_type=MESH)
    pl.semaphore_wait(barrier, nd - 1 + ntp - 1)

    def source(way, d):
        return z - d if way == 0 else z + d

    def has(way, d):
        return z >= d if way == 0 else z + d < nz

    def chunk_at(ref, first, k):
        return ref.at[pl.ds(pl.multiple_of(first + k * crow, crow), crow)]

    def nb_copy(way, d, k):
        first = (source(way, d) * 2 + c) * rows
        src = chunk_at(g_ref, 0, k) if d == 0 else chunk_at(g_all, first, k)
        return pltpu.make_async_remote_copy(
            src_ref=src, dst_ref=chunk_at(g_all, first, k),
            send_sem=nb_s.at[way, d, k], recv_sem=nb_r.at[way, d + 1, k],
            device_id=(dp, j + 2 if way == 0 else j - 2), device_id_type=MESH,
        )

    def nb_arrival(way, d, k):
        first = (source(way, d) * 2 + c) * rows
        here = chunk_at(g_all, first, k)
        return pltpu.make_async_remote_copy(
            src_ref=here, dst_ref=here,
            send_sem=nb_s.at[way, d, k], recv_sem=nb_r.at[way, d, k],
            device_id=(dp, sib), device_id_type=MESH,
        )

    def sib_copy(way, d, k, core):
        first = (source(way, d) * 2 + core) * rows
        src = chunk_at(g_ref, 0, k) if d == 0 else chunk_at(g_all, first, k)
        return pltpu.make_async_remote_copy(
            src_ref=src, dst_ref=chunk_at(g_all, first, k),
            send_sem=sib_s.at[way, d, k], recv_sem=sib_r.at[way, d, k],
            device_id=(dp, sib), device_id_type=MESH,
        )

    def send_on(way, d, k):
        @pl.when(has(way, d) & has(1 - way, 1))
        def _():
            nb_copy(way, d, k).start()

    def receive(d, k):
        for way in (0, 1):
            @pl.when(has(way, d))
            def _():
                nb_arrival(way, d, k).wait_recv()
            if d < nz - 1:
                send_on(way, d, k)

            @pl.when(has(way, d))
            def _():
                sib_copy(way, d, k, c).start()

    half = chunks // 2

    def send_own(lo, hi):
        for k in range(lo, hi):
            send_on(0, 0, k)
            send_on(1, 0, k)
            sib_copy(0, 0, k, c).start()

    send_own(0, half)

    def dp_copy(src, dst, s, r, k):
        return pltpu.make_async_remote_copy(
            src_ref=src, dst_ref=dst, send_sem=s.at[k], recv_sem=r.at[k],
            device_id=(dp_peer(k), j), device_id_type=MESH,
        )

    def tp_copy(src, dst, s, r, k):
        return pltpu.make_async_remote_copy(
            src_ref=src, dst_ref=dst, send_sem=s.at[k], recv_sem=r.at[k],
            device_id=(dp, tp_peer(k)), device_id_type=MESH,
        )

    def b_copy(k, who):
        return dp_copy(b_ref, b_all.at[pl.ds(who * held, held)], bdp_s, bdp_r, k)

    def a_copy(k, who):
        return dp_copy(a_ref, a_all.at[pl.ds(who * held, held)], adp_s, adp_r, k)

    for k in range(1, nd):
        b_copy(k, dp).start()
    for k in range(1, nd):
        a_copy(k, dp).start()

    def block_of(index):
        return lax.div(index * rows, block)

    own[1].wait()
    for k in range(1, nd):
        b_copy(k, dp_from(k)).wait_recv()
    for b in range(blocks):
        b_sel[b] = b_all[tab[dp, b]]
    b_in[j] = b_sel[block_of(j)]

    def bs_copy(k, who, whose):
        return tp_copy(b_sel.at[block_of(whose)], b_in.at[who], bs_s, bs_r, k)

    for k in range(1, ntp):
        bs_copy(k, j, tp_peer(k)).start()
    send_own(half, chunks)

    own[0].wait()
    for k in range(chunks):
        sib_copy(0, 0, k, 1 - c).wait_recv()

    def product(first, size, n):
        return dot_nt(g_all[pl.ds(first, size), :], w_v[slab(n, tile), :])

    def finish(zb, b, n, value):
        cols = slab(n, tile) if tiles > 1 else pl.ds(0, tile)
        filled = live[dp, b]
        keep = (lax.broadcasted_iota(jnp.int32, (block, 1), 0) < filled).astype(F32)
        extra = dot_nn(lo_t[b], a_sel[b, :, cols])
        hg_v[slab(b, block), cols] = (value * keep + adapter_scale * extra).astype(BF16)

    def mm_tiles(zb, lo, hi, final, wait_w):
        def one(n, carry):
            if wait_w:
                w_cp(n).wait()
            first = pl.multiple_of(zb * pair, pair)
            value = product(first, pair, n)
            if final:
                finish(zb, zb, n, value)
            else:
                cols = slab(n, tile) if tiles > 1 else pl.ds(0, tile)
                acc[pl.ds(first, pair), cols] = value
            return carry
        lax.fori_loop(lo, hi, one, 0)

    def fin_tiles(b):
        def one(n, carry):
            cols = slab(n, tile) if tiles > 1 else pl.ds(0, tile)
            finish(b, b, n, acc[slab(b, block), cols])
            return carry
        lax.fori_loop(0, tiles, one, 0)

    def hg_out(zb):
        return pltpu.make_async_copy(
            hg_v.at[slab(zb, block)], hg_ref.at[slab(zb, block)], out_sem.at[2 + zb]
        )

    def step(d, final, start=0, stop=chunks):
        def one(k, carry):
            if d + 1 < nz:
                receive(d + 1, k)
            lo, hi = lax.div(tiles * k, chunks), lax.div(tiles * (k + 1), chunks)
            for way in (0, 1) if d else (0,):
                @pl.when(has(way, d))
                def _():
                    mm_tiles(source(way, d), lo, hi, final, d == 0)
            return carry
        if start < stop:
            lax.fori_loop(start, stop, one, 0)
        if final and stop == chunks:
            for way in (0, 1) if d else (0,):
                @pl.when(has(way, d))
                def _():
                    hg_out(source(way, d)).start()

    def siblings(d):
        for way in (0, 1):
            @pl.when(has(way, d))
            def _():
                for k in range(chunks):
                    sib_copy(way, d, k, 1 - c).wait_recv()

    step(0, False, 0, half)

    for k in range(1, ntp):
        bs_copy(k, tp_from(k), j).wait_recv()
    low = jnp.zeros((rank, rows), F32)
    for s in range(ntp):
        low = low + dot_nt(b_in[s], g_all[slab(j, rows), s * feat : (s + 1) * feat])
    offset = lax.rem(j * rows, block)
    live_here = lax.broadcasted_iota(jnp.int32, (rank, rows), 1) + offset < live[dp, block_of(j)]
    low = (low * live_here.astype(F32)).astype(BF16)
    place = (
        lax.broadcasted_iota(jnp.int32, (rows, block), 1)
        == lax.broadcasted_iota(jnp.int32, (rows, block), 0) + offset
    ).astype(F32).astype(BF16)
    lo_all[j] = dot_nn(low, place).astype(BF16)

    def lo_copy(k, who):
        return tp_copy(lo_all.at[who], lo_all.at[who], lo_s, lo_r, k)

    for k in range(1, ntp):
        lo_copy(k, j).start()

    step(0, False, half)

    own[2].wait()
    for k in range(1, ntp):
        lo_copy(k, tp_from(k)).wait_recv()
    per_block = block // rows
    for b in range(blocks):
        value = lo_all[b * per_block].astype(F32)
        for s in range(1, per_block):
            value = value + lo_all[b * per_block + s].astype(F32)
        lo_bf[b] = value.astype(BF16)
        lo_t[b] = value.T.astype(BF16)
        ga[dp, b * rank : (b + 1) * rank, :] = (
            adapter_scale * dot_nn(lo_bf[b], h_v[b * block : (b + 1) * block, :])
        ).astype(BF16)

    def ga_copy(k, who):
        return dp_copy(ga.at[who], ga.at[who], ga_s, ga_r, k)

    def gb_copy(k, who):
        return dp_copy(gb.at[who], gb.at[who], gb_s, gb_r, k)

    for k in range(1, nd):
        ga_copy(k, dp).start()

    siblings(1)
    step(1, False, 0, half)

    own[3].wait()
    for k in range(1, nd):
        a_copy(k, dp_from(k)).wait_recv()
    for b in range(blocks):
        a_sel[b] = a_all[tab[dp, b]]
        value = dot_nt(a_sel[b], h_v[b * block : (b + 1) * block, :])
        for i in range(rank // piece):
            li_part[b * (rank // piece) + i] = value[i * piece : (i + 1) * piece, :]
    li_rs[j] = li_part[j]

    def rs_copy(k, who, whose):
        return tp_copy(li_part.at[whose], li_rs.at[who], rs_s, rs_r, k)

    for k in range(1, ntp):
        rs_copy(k, j, tp_peer(k)).start()

    step(1, False, half)

    for k in range(1, ntp):
        rs_copy(k, tp_from(k), j).wait_recv()
    total = li_rs[0]
    for s in range(1, ntp):
        total = total + li_rs[s]
    li_all[j] = total

    def li_copy(k, who):
        return tp_copy(li_all.at[who], li_all.at[who], li_s, li_r, k)

    for k in range(1, ntp):
        li_copy(k, j).start()

    if fused:
        for d in (0, 1):
            for way in (0, 1) if d else (0,):
                @pl.when(has(way, d))
                def _():
                    fin_tiles(source(way, d))
                    hg_out(source(way, d)).start()

    siblings(2)
    step(2, fused, 0, half)

    for k in range(1, ntp):
        li_copy(k, tp_from(k)).wait_recv()
    group = rank // piece
    for b in range(blocks):
        value = jnp.concatenate([li_all[b * group + i] for i in range(group)], axis=0)
        keep = lax.broadcasted_iota(jnp.int32, (rank, block), 1) < live[dp, b]
        li_bf[b] = (value * keep.astype(F32)).astype(BF16)

    def gb_block(b):
        gb[dp, slab(b, rank), :] = (
            adapter_scale * dot_nn(li_bf[b], g_all[slab(b, block), slab(j, feat)])
        ).astype(BF16)

    def gb_blocks(d):
        for way in (0, 1) if d else (0,):
            @pl.when(has(way, d))
            def _():
                gb_block(source(way, d))

    if fused:
        for d in range(nz - 1):
            gb_blocks(d)

    def chooser(g):
        r = lax.broadcasted_iota(jnp.int32, (held * rank, blocks * rank), 0)
        q = lax.broadcasted_iota(jnp.int32, (held * rank, blocks * rank), 1)
        same = (r & (rank - 1)) == (q & (rank - 1))
        which = jnp.zeros_like(q)
        for b in range(blocks):
            lane = (q >= b * rank) & (q < (b + 1) * rank)
            which = jnp.where(lane, tab[g, b] - dp * held, which)
        hit = (r >= which * rank) & (r < (which + 1) * rank) & same
        return hit.astype(F32).astype(BF16)

    picks = [chooser(g) for g in range(nd)]
    for k in range(1, nd):
        ga_copy(k, dp_from(k)).wait_recv()
    total = dot_nn(picks[0], ga[0])
    for g in range(1, nd):
        total = total + dot_nn(picks[g], ga[g])
    oa_v[...] = total.reshape(held, rank, ff)
    oa_cp = pltpu.make_async_copy(oa_v, oa_ref, out_sem.at[0])
    oa_cp.start()
    step(2, fused, half)
    for d in range(3, nz - 1):
        siblings(d)
        step(d, fused)

    siblings(nz - 1)
    if fused:
        gb_blocks(nz - 1)
    else:
        for b in range(blocks):
            gb_block(b)
    for k in range(1, nd):
        gb_copy(k, dp).start()

    step(nz - 1, fused)
    if not fused:
        for b in range(blocks):
            fin_tiles(b)
            hg_out(b).start()

    for k in range(1, nd):
        gb_copy(k, dp_from(k)).wait_recv()
    total = dot_nn(picks[0], gb[0])
    for g in range(1, nd):
        total = total + dot_nn(picks[g], gb[g])
    ob_v[...] = total.reshape(held, rank, feat)
    ob_cp = pltpu.make_async_copy(ob_v, ob_ref, out_sem.at[1])
    ob_cp.start()

    for d in range(nz):
        for way in (0, 1):
            if d < nz - 1:
                @pl.when(has(way, d) & has(1 - way, 1))
                def _():
                    for k in range(chunks):
                        nb_copy(way, d, k).wait_send()
            if d or way == 0:
                @pl.when(has(way, d))
                def _():
                    for k in range(chunks):
                        sib_copy(way, d, k, c).wait_send()
    for k in range(1, nd):
        for copy in (b_copy, a_copy, ga_copy, gb_copy):
            copy(k, dp).wait_send()
    for k in range(1, ntp):
        bs_copy(k, j, tp_peer(k)).wait_send()
        rs_copy(k, j, tp_peer(k)).wait_send()
        lo_copy(k, j).wait_send()
        li_copy(k, j).wait_send()
    for b in range(blocks):
        hg_out(b).wait()
    oa_cp.wait()
    ob_cp.wait()


def copy_kernel(blocks, hg, oa, ob, hg_out, oa_out, ob_out, hg_v, oa_v, ob_v, in_sem, out_sem):
    size = hg.shape[0] // blocks
    stages = [
        tuple(ref.at[pl.ds(b * size, size)] for ref in (hg, hg_v, hg_out)) for b in range(blocks)
    ] + [(oa, oa_v, oa_out), (ob, ob_v, ob_out)]
    loads = [pltpu.make_async_copy(s, v, in_sem.at[i]) for i, (s, v, _) in enumerate(stages)]
    stores = [pltpu.make_async_copy(v, o, out_sem.at[i]) for i, (_, v, o) in enumerate(stages)]
    for load in loads:
        load.start()
    for load, store in zip(loads, stores):
        load.wait()
        store.start()
    for store in stores:
        store.wait()


def shards(nd, ntp, g, h, w, a, bm, tab, live):
    blocks = tab.shape[1]
    group_rows, ff = h.shape
    block = group_rows // blocks
    held, rank, _ = a.shape
    feat = bm.shape[2]
    rows, width = g.shape
    nz = ntp // 2
    chunks = max(1, min(2, rows // 16))
    tiles = ff // 256 if ff % 256 == 0 else 1
    piece = blocks * rank // ntp
    V = pltpu.VMEM
    dma = lambda *s: pltpu.SemaphoreType.DMA(s)
    scratch = [
        V((group_rows, width), BF16), V((group_rows, ff), BF16), V((ff, width), BF16),
        V((nd * held, rank, ff), BF16), V((nd * held, rank, feat), BF16),
        V((blocks, rank, ff), BF16), V((blocks, rank, feat), BF16),
        V((ntp, rank, feat), BF16), V((ntp, rank, block), BF16),
        V((blocks, rank, block), BF16), V((blocks, block, rank), BF16),
        V((ntp, piece, block), F32), V((ntp, piece, block), F32), V((ntp, piece, block), F32),
        V((blocks, rank, block), BF16),
        V((nd, blocks * rank, ff), BF16), V((nd, blocks * rank, feat), BF16),
        V((group_rows, ff), F32), V((group_rows, ff), BF16),
        V((held, rank, ff), F32), V((held, rank, feat), F32),
        dma(tiles), dma(4), dma(2 + blocks),
        dma(2, nz, chunks), dma(2, nz + 1, chunks), dma(2, nz, chunks), dma(2, nz, chunks),
        dma(nd), dma(nd), dma(nd), dma(nd), dma(ntp), dma(ntp),
        dma(ntp), dma(ntp), dma(ntp), dma(ntp), dma(ntp), dma(ntp),
        dma(nd), dma(nd), dma(nd), dma(nd),
    ]
    any_spec = pl.BlockSpec(memory_space=pl.ANY)
    smem = pl.BlockSpec(memory_space=pltpu.SMEM)
    hg, oa, ob = pl.pallas_call(
        functools.partial(
            kernel, nd, ntp, blocks, block, rank, held, rows, chunks, ff, feat, tiles
        ),
        out_shape=(
            jax.ShapeDtypeStruct((group_rows, ff), BF16),
            jax.ShapeDtypeStruct((held, rank, ff), F32),
            jax.ShapeDtypeStruct((held, rank, feat), F32),
        ),
        in_specs=[any_spec] * 5 + [smem] * 2,
        out_specs=(any_spec,) * 3,
        scratch_shapes=scratch,
        compiler_params=pltpu.CompilerParams(
            collective_id=0, has_side_effects=True, vmem_limit_bytes=62 * 1024 * 1024
        ),
    )(g, h, w, a, bm, tab, live)
    results = (hg, oa, ob)
    return pl.pallas_call(
        functools.partial(copy_kernel, blocks),
        out_shape=tuple(jax.ShapeDtypeStruct(x.shape, x.dtype) for x in results),
        in_specs=[any_spec] * 3,
        out_specs=(any_spec,) * 3,
        scratch_shapes=[V(x.shape, x.dtype) for x in results] + [dma(blocks + 2), dma(blocks + 2)],
        compiler_params=pltpu.CompilerParams(vmem_limit_bytes=62 * 1024 * 1024),
    )(*results)


def solution(mesh):
    in_specs = (
        P(("dp", "seqtp"), None),
        P("dp", "seqtp"),
        P("seqtp", None),
        P("dp", None, "seqtp"),
        P("dp", None, "seqtp"),
        P(),
        P(),
    )
    out_specs = (P("dp", "seqtp"), P("dp", None, "seqtp"), P("dp", None, "seqtp"))
    body = functools.partial(shards, mesh.shape["dp"], mesh.shape["seqtp"])
    return jax.shard_map(body, mesh=mesh, in_specs=in_specs, out_specs=out_specs, check_vma=False)
```

profile of v0, /device:TPU:0, one launch (start us, length us, event | category | flops | bytes accessed | tf_op | source)
XLA Modules:
  0.0 62.0 jit_solution(18107131590178174748)
XLA Ops:
  0.6 58.7 %shard_map.94 = (bf16[512,1792]{1,0:T(8,128)(2,1)}, f32[6,16,1792]{2,1,0:T(8,128)}, f32[6,16,512]{2,1,0:T(8,128)}) custom-call(bf16[64,4096]{1,0:T(8,128)(2,1)} %g_ref.1, bf16[512,1792]{1,0:T(8,128)(2,1)} %h_ref.1, bf16[1792,4096]{1,0:T(8,128)(2,1)} %w_ref.1, bf16[6,16,1792]{2,1,0:T(8,128)(2,1)} %a_ref.1, bf16[6,16,512]{2,1,0:T(8,128)(2,1)} %b_ref.1, ...), custom_call_target="tpu_custom_call" | custom-call | tf_op jit(solution)/shard_map/pallas_call | solution.py:490
  59.3 2.7 %shard_map.95 = (bf16[512,1792]{1,0:T(8,128)(2,1)}, f32[6,16,1792]{2,1,0:T(8,128)}, f32[6,16,512]{2,1,0:T(8,128)}) custom-call(bf16[512,1792]{1,0:T(8,128)(2,1)} %get-tuple-element.6.hg, f32[6,16,1792]{2,1,0:T(8,128)} %get-tuple-element.7.oa, f32[6,16,512]{2,1,0:T(8,128)} %get-tuple-element.8.ob), custom_call_target="tpu_custom_call" | custom-call | tf_op jit(solution)/shard_map/pallas_call | solution.py:507
where the time goes:
time: 62.2 us; the launch traced here: 62 us
  Pallas kernels  61.4 us (99%)
  between operations  0.64 us (1%)
    pallas_call x1, Pallas kernels, shards(): pl.pallas_call(functools.partial(kernel, nd, ntp, blocks, block, rank, he...  58.7 us
    pallas_call x1, Pallas kernels, shards(): pl.pallas_call(functools.partial(copy_kernel, blocks), out_shape=tuple((j...  2.66 us

commit v1 on v0

--- a/solution.py
+++ b/solution.py
@@ -514,6 +514,514 @@
     )(*results)
 
 
+def line_kernel(
+    nd, nz, blocks, block, rank, held, rows, sizes, ff, feat, width,
+    g_ref, h_ref, w_ref, a_ref, b_ref, tab, live,
+    hg_v, oa_v, ob_v,
+    g_all, h_v, w_v, a_all, b_all, a_sel, b_sel, b_in, lo_part, lo_all, lo_t,
+    li_part, li_sib, li_sum, li_rs, li_all, ga, gb, acc,
+    w_sem, own_sem, relay,
+    nb_s, nb_r, sib_s, sib_r, row_s, row_r, bdp_s, bdp_r, adp_s, adp_r,
+    bs_s, bs_r, lo_s, lo_r, rs_s, rs_r, ag_s, ag_r, pair_s, pair_r,
+    ga_s, ga_r, gb_s, gb_r,
+):
+    dp = lax.axis_index("dp")
+    j = lax.axis_index("seqtp")
+    z = lax.div(j, 2)
+    c = lax.rem(j, 2)
+    sib = z * 2 + 1 - c
+    chunks = len(sizes)
+    tile = 256
+    tiles = ff // tile
+    piece = blocks * rank // (2 * nz)
+    pair_rows = 2 * block
+    near = lax.div(z, 2)
+    far = 1 - near
+    starts = [sum(sizes[:i]) for i in range(chunks)]
+
+    def slab(index, size):
+        return pl.ds(pl.multiple_of(index * size, size), size)
+
+    def has(way, d):
+        return z >= d if way == 0 else z + d < nz
+
+    def source(way, d):
+        return z - d if way == 0 else z + d
+
+    def dp_peer(k):
+        return lax.rem(dp + k, nd)
+
+    def dp_from(k):
+        return lax.rem(dp + nd - k, nd)
+
+    def z_peer(k):
+        return lax.rem(z + k, nz)
+
+    def z_from(k):
+        return lax.rem(z + nz - k, nz)
+
+    def toward(way):
+        return (dp, j + 2 if way == 0 else j - 2)
+
+    barrier = pltpu.get_barrier_semaphore()
+    for way in (0, 1):
+        @pl.when(has(1 - way, 1))
+        def _():
+            pl.semaphore_signal(barrier, inc=1, device_id=toward(way), device_id_type=MESH)
+    pl.semaphore_signal(barrier, inc=1, device_id=(dp, sib), device_id_type=MESH)
+    for k in range(1, nd):
+        pl.semaphore_signal(barrier, inc=1, device_id=(dp_peer(k), j), device_id_type=MESH)
+
+    own = [
+        pltpu.make_async_copy(b_ref, b_all.at[pl.ds(dp * held, held)], own_sem.at[0]),
+        pltpu.make_async_copy(g_ref, g_all.at[slab(j, rows)], own_sem.at[1]),
+        pltpu.make_async_copy(h_ref, h_v, own_sem.at[2]),
+        pltpu.make_async_copy(a_ref, a_all.at[pl.ds(dp * held, held)], own_sem.at[3]),
+    ]
+    w_cp = [
+        pltpu.make_async_copy(w_ref.at[pl.ds(n * tile, tile)], w_v.at[pl.ds(n * tile, tile)], w_sem.at[n])
+        for n in range(tiles)
+    ]
+    own[0].start()
+    own[1].start()
+
+    @pl.when(has(0, 1) & has(1, 1))
+    def _():
+        pl.semaphore_wait(barrier, nd + 2)
+
+    @pl.when(jnp.logical_not(has(0, 1) & has(1, 1)))
+    def _():
+        pl.semaphore_wait(barrier, nd + 1)
+
+    def part(ref, first, way, i):
+        start = starts[i] if way == 1 else width - starts[i] - sizes[i]
+        return ref.at[slab(first, rows), pl.ds(start, sizes[i])]
+
+    def nb_copy(way, d, i):
+        first = source(way, d) * 2 + c
+        src = part(g_ref, 0, way, i) if d == 0 else part(g_all, first, way, i)
+        return pltpu.make_async_remote_copy(
+            src_ref=src, dst_ref=part(g_all, first, way, i),
+            send_sem=nb_s.at[way, d, i], recv_sem=nb_r.at[way, d + 1, i],
+            device_id=toward(way), device_id_type=MESH,
+        )
+
+    def nb_arrival(way, d, i):
+        here = part(g_all, source(way, d) * 2 + c, way, i)
+        return pltpu.make_async_remote_copy(
+            src_ref=here, dst_ref=here,
+            send_sem=nb_s.at[way, d - 1, i], recv_sem=nb_r.at[way, d, i],
+            device_id=(dp, sib), device_id_type=MESH,
+        )
+
+    def sib_copy(way, d, i, core):
+        here = part(g_all, source(way, d) * 2 + core, way, i)
+        return pltpu.make_async_remote_copy(
+            src_ref=here, dst_ref=here,
+            send_sem=sib_s.at[way, d, i], recv_sem=sib_r.at[way, d, i],
+            device_id=(dp, sib), device_id_type=MESH,
+        )
+
+    def row_copy(index):
+        return pltpu.make_async_remote_copy(
+            src_ref=g_ref, dst_ref=g_all.at[slab(index, rows)],
+            send_sem=row_s, recv_sem=row_r, device_id=(dp, sib), device_id_type=MESH,
+        )
+
+    def send_own(lo, hi):
+        for i in range(lo, hi):
+            for way in (0, 1):
+                @pl.when(has(1 - way, 1))
+                def _():
+                    nb_copy(way, 0, i).start()
+
+    def event(n):
+        d, i = n // chunks + 1, n % chunks
+        for way in (0, 1):
+            @pl.when(has(way, d))
+            def _():
+                nb_arrival(way, d, i).wait_recv()
+                if d < nz - 1:
+                    @pl.when(has(1 - way, 1))
+                    def _():
+                        nb_copy(way, d, i).start()
+                sib_copy(way, d, i, c).start()
+
+    def landed(n):
+        d, i = n // chunks + 1, n % chunks
+        for way in (0, 1):
+            @pl.when(has(way, d))
+            def _():
+                sib_copy(way, d, i, 1 - c).wait_recv()
+
+    def dp_copy(src, dst, s, r, k):
+        return pltpu.make_async_remote_copy(
+            src_ref=src, dst_ref=dst, send_sem=s.at[k], recv_sem=r.at[k],
+            device_id=(dp_peer(k), j), device_id_type=MESH,
+        )
+
+    def z_copy(src, dst, s, r, k):
+        return pltpu.make_async_remote_copy(
+            src_ref=src, dst_ref=dst, send_sem=s.at[k], recv_sem=r.at[k],
+            device_id=(dp, z_peer(k) * 2 + c), device_id_type=MESH,
+        )
+
+    def core_copy(src, dst, k):
+        return pltpu.make_async_remote_copy(
+            src_ref=src, dst_ref=dst, send_sem=pair_s.at[k], recv_sem=pair_r.at[k],
+            device_id=(dp, sib), device_id_type=MESH,
+        )
+
+    def b_copy(k, who):
+        return dp_copy(b_ref, b_all.at[pl.ds(who * held, held)], bdp_s, bdp_r, k)
+
+    def a_copy(k, who):
+        return dp_copy(a_ref, a_all.at[pl.ds(who * held, held)], adp_s, adp_r, k)
+
+    def bs_copy(k, who, whose):
+        return z_copy(b_sel.at[whose], b_in.at[who], bs_s, bs_r, k)
+
+    def lo_copy(k, who):
+        return z_copy(lo_all.at[who], lo_all.at[who], lo_s, lo_r, k)
+
+    def rs_copy(k, who, whose):
+        return z_copy(li_sum.at[whose], li_rs.at[who], rs_s, rs_r, k)
+
+    def ag_copy(k, who):
+        return z_copy(li_all.at[c * nz + who], li_all.at[c * nz + who], ag_s, ag_r, k)
+
+    def ga_copy(k, who):
+        return dp_copy(ga.at[who], ga.at[who], ga_s, ga_r, k)
+
+    def gb_copy(k, who):
+        return dp_copy(gb.at[who], gb.at[who], gb_s, gb_r, k)
+
+    def lo_pair(core):
+        return core_copy(lo_part.at[core], lo_part.at[core], 0)
+
+    def li_pair(core):
+        return core_copy(li_part.at[1 - core], li_sib, 1)
+
+    def ag_pair(core):
+        here = li_all.at[pl.ds(core * nz, nz)]
+        return core_copy(here, here, 2)
+
+    half = chunks // 2
+    send_own(0, half)
+    for k in range(1, nd):
+        b_copy(k, dp).start()
+    row_copy(j).start()
+    for way in (0, 1):
+        @pl.when(has(way, 1) & has(1 - way, 1))
+        def _():
+            pl.semaphore_signal(relay.at[way, 2], inc=1, device_id=toward(way), device_id_type=MESH)
+    for n in range(tiles):
+        w_cp[n].start()
+    own[2].start()
+    own[3].start()
+    for k in range(1, nd):
+        a_copy(k, dp).start()
+    send_own(half, chunks)
+
+    for d in range(2, nz):
+        for way in (0, 1):
+            @pl.when(has(way, d))
+            def _():
+                pl.semaphore_wait(relay.at[way, d], 1)
+                if d + 1 < nz:
+                    @pl.when(has(1 - way, 1))
+                    def _():
+                        pl.semaphore_signal(
+                            relay.at[way, d + 1], inc=1, device_id=toward(way), device_id_type=MESH
+                        )
+
+    own[0].wait()
+    for k in range(1, nd):
+        b_copy(k, dp_from(k)).wait_recv()
+    for b in range(blocks):
+        b_sel[b] = b_all[tab[dp, b]]
+    b_in[z] = b_sel[z]
+    for k in range(1, nz):
+        bs_copy(k, z, z_peer(k)).start()
+
+    event(0)
+
+    own[1].wait()
+    row_copy(sib).wait_recv()
+    for k in range(1, nz):
+        bs_copy(k, z_from(k), z).wait_recv()
+    low = jnp.zeros((rank, block), F32)
+    for s in range(nz):
+        low = low + dot_nt(b_in[s], g_all[slab(z, block), slab(2 * s + c, feat)])
+    lo_part[c] = low
+    lo_pair(c).start()
+
+    event(1)
+
+    lo_pair(1 - c).wait_recv()
+    lanes = lax.broadcasted_iota(jnp.int32, (rank, block), 1)
+    low = lo_part[0] + lo_part[1]
+    lo_all[z] = (low * (lanes < live[dp, z]).astype(F32)).astype(BF16)
+    for k in range(1, nz):
+        lo_copy(k, z).start()
+
+    event(2)
+
+    own[3].wait()
+    for k in range(1, nd):
+        a_copy(k, dp_from(k)).wait_recv()
+    own[2].wait()
+    for b in range(blocks):
+        a_sel[b] = a_all[tab[dp, b]]
+        value = dot_nt(a_sel[b], h_v[b * block : (b + 1) * block, :])
+        for i in range(rank // piece):
+            at = b * (rank // piece) + i
+            li_part[at // nz, at % nz] = value[i * piece : (i + 1) * piece, :]
+    li_pair(c).start()
+    for k in range(1, nz):
+        lo_copy(k, z_from(k)).wait_recv()
+    for b in range(blocks):
+        lo_t[b] = lo_all[b].astype(F32).T.astype(BF16)
+        ga[dp, b * rank : (b + 1) * rank, :] = (
+            adapter_scale * dot_nn(lo_all[b], h_v[b * block : (b + 1) * block, :])
+        ).astype(BF16)
+    for k in range(1, nd):
+        ga_copy(k, dp).start()
+
+    event(3)
+
+    li_pair(1 - c).wait_recv()
+    li_sum[...] = li_part[c] + li_sib[...]
+    li_rs[z] = li_sum[z]
+    for k in range(1, nz):
+        rs_copy(k, z, z_peer(k)).start()
+
+    def keep_of(b):
+        return (lax.broadcasted_iota(jnp.int32, (block, 1), 0) < live[dp, b]).astype(F32)
+
+    for n in range(chunks):
+        landed(n)
+    for n in range(tiles):
+        w_cp[n].wait()
+
+    def near_tiles(lo, hi):
+        def one(n, carry):
+            cols = slab(n, tile)
+            value = dot_nt(g_all[slab(near, pair_rows), :], w_v[slab(n, tile), :])
+            for s in range(2):
+                b = near * 2 + s
+                extra = dot_nn(lo_t[b], a_sel[b, :, cols])
+                total = value[s * block : (s + 1) * block] + adapter_scale * extra
+                hg_v[slab(b, block), cols] = (total * keep_of(b)).astype(BF16)
+            return carry
+        lax.fori_loop(lo, hi, one, 0)
+
+    near_tiles(0, tiles // 3)
+    event(chunks)
+
+    for k in range(1, nz):
+        rs_copy(k, z_from(k), z).wait_recv()
+    total = li_rs[0]
+    for s in range(1, nz):
+        total = total + li_rs[s]
+    whole = c * nz + z
+    lanes = lax.broadcasted_iota(jnp.int32, (piece, block), 1)
+    filled = live[dp, lax.div(whole * piece, rank)]
+    li_all[whole] = (total * (lanes < filled).astype(F32)).astype(BF16)
+    for k in range(1, nz):
+        ag_copy(k, z).start()
+
+    near_tiles(tiles // 3, 2 * tiles // 3)
+    event(chunks + 1)
+    for k in range(1, nz):
+        ag_copy(k, z_from(k)).wait_recv()
+    ag_pair(c).start()
+    near_tiles(2 * tiles // 3, tiles)
+    event(chunks + 2)
+
+    ag_pair(1 - c).wait_recv()
+
+    def gb_block(b):
+        group = rank // piece
+        rows_of = jnp.concatenate(
+            [li_all[b * group + i].astype(F32) for i in range(group)], axis=0
+        ).astype(BF16)
+        gb[dp, slab(b, rank), :] = (
+            adapter_scale * dot_nn(rows_of, g_all[slab(b, block), slab(j, feat)])
+        ).astype(BF16)
+
+    for s in range(2):
+        gb_block(near * 2 + s)
+
+    def chooser(g):
+        r = lax.broadcasted_iota(jnp.int32, (held * rank, blocks * rank), 0)
+        q = lax.broadcasted_iota(jnp.int32, (held * rank, blocks * rank), 1)
+        same = (r & (rank - 1)) == (q & (rank - 1))
+        which = jnp.zeros_like(q)
+        for b in range(blocks):
+            lane = (q >= b * rank) & (q < (b + 1) * rank)
+            which = jnp.where(lane, tab[g, b] - dp * held, which)
+        hit = (r >= which * rank) & (r < (which + 1) * rank) & same
+        return hit.astype(F32).astype(BF16)
+
+    def owned(ref):
+        total = dot_nn(chooser(0), ref[0])
+        for g in range(1, nd):
+            total = total + dot_nn(chooser(g), ref[g])
+        return total
+
+    for k in range(1, nd):
+        ga_copy(k, dp_from(k)).wait_recv()
+    oa_v[...] = owned(ga).reshape(held, rank, ff)
+
+    for n in range(chunks + 3, 2 * chunks):
+        event(n)
+    for s in range(2):
+        b = far * 2 + s
+        acc[s * block : (s + 1) * block, :] = adapter_scale * dot_nn(lo_t[b], a_sel[b])
+
+    def drain(d):
+        for way in (0, 1):
+            for i in range(chunks):
+                if d < nz - 1:
+                    @pl.when(has(way, d) & has(1 - way, 1))
+                    def _():
+                        nb_copy(way, d, i).wait_send()
+                if d:
+                    @pl.when(has(way, d))
+                    def _():
+                        sib_copy(way, d, i, c).wait_send()
+
+    row_copy(j).wait_send()
+    drain(0)
+    drain(1)
+    for k in range(1, nd):
+        for copy in (b_copy, a_copy, ga_copy):
+            copy(k, dp).wait_send()
+    for k in range(1, nz):
+        bs_copy(k, z, z_peer(k)).wait_send()
+        lo_copy(k, z).wait_send()
+        rs_copy(k, z, z_peer(k)).wait_send()
+        ag_copy(k, z).wait_send()
+    for copy in (lo_pair, li_pair, ag_pair):
+        copy(c).wait_send()
+    for n in range(chunks, 2 * chunks):
+        landed(n)
+
+    def far_chunk(i, last):
+        start = jnp.where(z < nz // 2, starts[i], width - starts[i] - sizes[i])
+        deep = pl.ds(pl.multiple_of(start, 128), sizes[i])
+        keep = jnp.concatenate([keep_of(far * 2 + s) for s in range(2)], axis=0) if last else None
+        rows_at = slab(far, pair_rows)
+        for n in range(tiles):
+            cols = pl.ds(n * tile, tile)
+            value = acc[:, cols] + dot_nt(g_all[rows_at, deep], w_v[cols, deep])
+            if last:
+                hg_v[rows_at, cols] = (value * keep).astype(BF16)
+            else:
+                acc[:, cols] = value
+
+    for i in range(chunks):
+        event(2 * chunks + i)
+        landed(2 * chunks + i)
+        far_chunk(i, i == chunks - 1)
+        if i == 0:
+            for s in range(2):
+                gb_block(far * 2 + s)
+            for k in range(1, nd):
+                gb_copy(k, dp).start()
+        if i == chunks - 2:
+            for k in range(1, nd):
+                gb_copy(k, dp_from(k)).wait_recv()
+            ob_v[...] = owned(gb).reshape(held, rank, feat)
+            for k in range(1, nd):
+                gb_copy(k, dp).wait_send()
+            drain(2)
+    for d in range(3, nz):
+        drain(d)
+
+
+def store_kernel(blocks, hg, oa, ob, hg_out, oa_out, ob_out, sem):
+    size = hg.shape[0] // blocks
+    copies = [
+        (hg.at[pl.ds(b * size, size)], hg_out.at[pl.ds(b * size, size)]) for b in range(blocks)
+    ] + [(oa, oa_out), (ob, ob_out)]
+    copies = [pltpu.make_async_copy(s, o, sem.at[i]) for i, (s, o) in enumerate(copies)]
+    for copy in copies:
+        copy.start()
+    for copy in copies:
+        copy.wait()
+
+
+def line_shards(nd, ntp, g, h, w, a, bm, tab, live):
+    blocks = tab.shape[1]
+    group_rows, ff = h.shape
+    block = group_rows // blocks
+    held, rank, _ = a.shape
+    feat = bm.shape[2]
+    rows, width = g.shape
+    nz = ntp // 2
+    sizes = (width // 4,) * 4
+    tiles = ff // 256
+    chunks = len(sizes)
+    piece = blocks * rank // ntp
+    V = pltpu.VMEM
+    dma = lambda *s: pltpu.SemaphoreType.DMA(s)
+    scratch = [
+        V((group_rows, width), BF16), V((group_rows, ff), BF16), V((ff, width), BF16),
+        V((nd * held, rank, ff), BF16), V((nd * held, rank, feat), BF16),
+        V((blocks, rank, ff), BF16), V((blocks, rank, feat), BF16), V((nz, rank, feat), BF16),
+        V((2, rank, block), F32), V((blocks, rank, block), BF16), V((blocks, block, rank), BF16),
+        V((2, nz, piece, block), F32), V((nz, piece, block), F32), V((nz, piece, block), F32),
+        V((nz, piece, block), F32), V((ntp, piece, block), BF16),
+        V((nd, blocks * rank, ff), BF16), V((nd, blocks * rank, feat), BF16),
+        V((2 * block, ff), F32),
+        dma(tiles), dma(4), pltpu.SemaphoreType.REGULAR((2, nz)),
+        dma(2, nz, chunks), dma(2, nz + 1, chunks), dma(2, nz, chunks), dma(2, nz, chunks),
+        pltpu.SemaphoreType.DMA, pltpu.SemaphoreType.DMA,
+        dma(nd), dma(nd), dma(nd), dma(nd),
+        dma(nz), dma(nz), dma(nz), dma(nz), dma(nz), dma(nz), dma(nz), dma(nz), dma(3), dma(3),
+        dma(nd), dma(nd), dma(nd), dma(nd),
+    ]
+    hbm = pl.BlockSpec(memory_space=pltpu.HBM)
+    smem = pl.BlockSpec(memory_space=pltpu.SMEM)
+    vmem = pl.BlockSpec(memory_space=pltpu.VMEM)
+    results = pl.pallas_call(
+        functools.partial(
+            line_kernel, nd, nz, blocks, block, rank, held, rows, sizes, ff, feat, width
+        ),
+        out_shape=(
+            V((group_rows, ff), BF16), V((held, rank, ff), F32), V((held, rank, feat), F32),
+        ),
+        in_specs=[hbm] * 5 + [smem] * 2,
+        out_specs=(vmem,) * 3,
+        scratch_shapes=scratch,
+        compiler_params=pltpu.CompilerParams(
+            collective_id=1, has_side_effects=True, vmem_limit_bytes=61 * 1024 * 1024
+        ),
+    )(g, h, w, a, bm, tab, live)
+    return pl.pallas_call(
+        functools.partial(store_kernel, blocks),
+        out_shape=tuple(jax.ShapeDtypeStruct(x.shape, x.dtype) for x in results),
+        in_specs=[vmem] * 3,
+        out_specs=(hbm,) * 3,
+        scratch_shapes=[dma(blocks + 2)],
+        compiler_params=pltpu.CompilerParams(vmem_limit_bytes=8 * 1024 * 1024),
+    )(*results)
+
+
+def body(nd, ntp, g, h, w, a, bm, tab, live):
+    blocks = tab.shape[1]
+    group_rows, ff = h.shape
+    rows, width = g.shape
+    line = (
+        ntp == 8 and blocks == 4 and 8 * rows == group_rows and ff % 256 == 0
+        and width == ntp * bm.shape[2] and bm.shape[2] % 128 == 0
+        and blocks * a.shape[1] == 8 * ntp
+    )
+    return (line_shards if line else shards)(nd, ntp, g, h, w, a, bm, tab, live)
+
+
 def solution(mesh):
     in_specs = (
         P(("dp", "seqtp"), None),
@@ -525,5 +1033,5 @@
         P(),
     )
     out_specs = (P("dp", "seqtp"), P("dp", None, "seqtp"), P("dp", None, "seqtp"))
-    body = functools.partial(shards, mesh.shape["dp"], mesh.shape["seqtp"])
-    return jax.shard_map(body, mesh=mesh, in_specs=in_specs, out_specs=out_specs, check_vma=False)
+    step = functools.partial(body, mesh.shape["dp"], mesh.shape["seqtp"])
+    return jax.shard_map(step, mesh=mesh, in_specs=in_specs, out_specs=out_specs, check_vma=False)

time: 62.2 us -> 54.6 us (0.88)
  Pallas kernels: 61.4 us -> 53.3 us
    pallas_call x2, Pallas kernels: 61.4 us -> 53.3 us  [the longest x1 51.8 us: line_shards(): pl.pallas_call(functools.partial(line_kernel, nd, nz, blocks, block, rank...]
where the time goes in v1:
time: 54.6 us; the launch traced here: 54 us
  Pallas kernels  53.3 us (98%)
  between operations  0.64 us (1%)
    pallas_call x1, Pallas kernels, line_shards(): pl.pallas_call(functools.partial(line_kernel, nd, nz, blocks, block, rank...  51.8 us
    pallas_call x1, Pallas kernels, line_shards(): pl.pallas_call(functools.partial(store_kernel, blocks), out_shape=tuple((...  1.56 us

profile of v1, /device:TPU:0, one launch (start us, length us, event | category | flops | bytes accessed | tf_op | source)
XLA Modules:
  0.0 54.0 jit_solution(18347539537218661267)
XLA Ops:
  0.6 51.8 %shard_map.94 = (bf16[512,1792]{1,0:T(8,128)(2,1)S(1)}, f32[6,16,1792]{2,1,0:T(8,128)S(1)}, f32[6,16,512]{2,1,0:T(8,128)S(1)}) custom-call(bf16[64,4096]{1,0:T(8,128)(2,1)} %g_ref.1, bf16[512,1792]{1,0:T(8,128)(2,1)} %h_ref.1, bf16[1792,4096]{1,0:T(8,128)(2,1)} %w_ref.1, bf16[6,16,1792]{2,1,0:T(8,128)(2,1)} %a_ref.1, bf16[6,16,512]{2,1,0:T(8,128)(2,1)} %b_ref.1, ...), custom_call_target="tpu_custom_call" | custom-call | tf_op jit(solution)/shard_map/pallas_call | solution.py:989
  52.4 1.6 %shard_map.95 = (bf16[512,1792]{1,0:T(8,128)(2,1)}, f32[6,16,1792]{2,1,0:T(8,128)}, f32[6,16,512]{2,1,0:T(8,128)}) custom-call(bf16[512,1792]{1,0:T(8,128)(2,1)S(1)} %get-tuple-element.6.hg, f32[6,16,1792]{2,1,0:T(8,128)S(1)} %get-tuple-element.7.oa, f32[6,16,512]{2,1,0:T(8,128)S(1)} %get-tuple-element.8.ob), custom_call_target="tpu_custom_call" | custom-call | tf_op jit(solution)/shard_map/pallas_call | solution.py:1003

commit v2 on v1

--- a/solution.py
+++ b/solution.py
@@ -518,8 +518,8 @@
     nd, nz, blocks, block, rank, held, rows, sizes, ff, feat, width,
     g_ref, h_ref, w_ref, a_ref, b_ref, tab, live,
     hg_v, oa_v, ob_v,
-    g_all, h_v, w_v, a_all, b_all, a_sel, b_sel, b_in, lo_part, lo_all, lo_t,
-    li_part, li_sib, li_sum, li_rs, li_all, ga, gb, acc,
+    g_all, h_v, w_v, a_own, b_own, a_out, b_out, a_in, b_from, a_sel, b_sel, b_in,
+    lo_part, lo_all, lo_t, li_part, li_sib, li_sum, li_rs, li_all, ga, gb, acc,
     w_sem, own_sem, relay,
     nb_s, nb_r, sib_s, sib_r, row_s, row_r, bdp_s, bdp_r, adp_s, adp_r,
     bs_s, bs_r, lo_s, lo_r, rs_s, rs_r, ag_s, ag_r, pair_s, pair_r,
@@ -573,16 +573,17 @@
         pl.semaphore_signal(barrier, inc=1, device_id=(dp_peer(k), j), device_id_type=MESH)
 
     own = [
-        pltpu.make_async_copy(b_ref, b_all.at[pl.ds(dp * held, held)], own_sem.at[0]),
+        pltpu.make_async_copy(b_ref, b_own, own_sem.at[0]),
         pltpu.make_async_copy(g_ref, g_all.at[slab(j, rows)], own_sem.at[1]),
         pltpu.make_async_copy(h_ref, h_v, own_sem.at[2]),
-        pltpu.make_async_copy(a_ref, a_all.at[pl.ds(dp * held, held)], own_sem.at[3]),
+        pltpu.make_async_copy(a_ref, a_own, own_sem.at[3]),
     ]
     w_cp = [
         pltpu.make_async_copy(w_ref.at[pl.ds(n * tile, tile)], w_v.at[pl.ds(n * tile, tile)], w_sem.at[n])
         for n in range(tiles)
     ]
     own[0].start()
+    own[3].start()
     own[1].start()
 
     @pl.when(has(0, 1) & has(1, 1))
@@ -628,24 +629,28 @@
             send_sem=row_s, recv_sem=row_r, device_id=(dp, sib), device_id_type=MESH,
         )
 
-    def send_own(lo, hi):
-        for i in range(lo, hi):
+    def onward(way, d):
+        return has(way, d) & has(1 - way, 1)
+
+    def advance(n):
+        d, i = n // chunks, n % chunks
+        if d < nz - 1:
             for way in (0, 1):
-                @pl.when(has(1 - way, 1))
+                @pl.when(onward(way, d))
                 def _():
-                    nb_copy(way, 0, i).start()
+                    nb_copy(way, d, i).start()
 
     def event(n):
-        d, i = n // chunks + 1, n % chunks
+        d, i = n // chunks, n % chunks
         for way in (0, 1):
-            @pl.when(has(way, d))
+            @pl.when(has(way, d + 1))
             def _():
-                nb_arrival(way, d, i).wait_recv()
-                if d < nz - 1:
-                    @pl.when(has(1 - way, 1))
-                    def _():
-                        nb_copy(way, d, i).start()
-                sib_copy(way, d, i, c).start()
+                nb_arrival(way, d + 1, i).wait_recv()
+                sib_copy(way, d + 1, i, c).start()
+        for way in (0, 1):
+            @pl.when(onward(way, d))
+            def _():
+                nb_copy(way, d, i).wait_send()
 
     def landed(n):
         d, i = n // chunks + 1, n % chunks
@@ -673,10 +678,13 @@
         )
 
     def b_copy(k, who):
-        return dp_copy(b_ref, b_all.at[pl.ds(who * held, held)], bdp_s, bdp_r, k)
+        return dp_copy(b_out.at[k], b_from.at[who], bdp_s, bdp_r, k)
 
     def a_copy(k, who):
-        return dp_copy(a_ref, a_all.at[pl.ds(who * held, held)], adp_s, adp_r, k)
+        return dp_copy(a_out.at[k], a_in.at[who], adp_s, adp_r, k)
+
+    def at_owner(group, b):
+        return jnp.clip(tab[group, b] - dp * held, 0, held - 1)
 
     def bs_copy(k, who, whose):
         return z_copy(b_sel.at[whose], b_in.at[who], bs_s, bs_r, k)
@@ -706,22 +714,31 @@
         here = li_all.at[pl.ds(core * nz, nz)]
         return core_copy(here, here, 2)
 
-    half = chunks // 2
-    send_own(0, half)
-    for k in range(1, nd):
+    advance(0)
+    advance(1)
+    advance(2)
+    row_copy(j).start()
+    own[0].wait()
+    for k in range(1, nd):
+        for b in range(blocks):
+            b_out[k, b] = b_own[at_owner(dp_peer(k), b)]
         b_copy(k, dp).start()
-    row_copy(j).start()
+    for b in range(blocks):
+        b_from[dp, b] = b_own[at_owner(dp, b)]
     for way in (0, 1):
         @pl.when(has(way, 1) & has(1 - way, 1))
         def _():
             pl.semaphore_signal(relay.at[way, 2], inc=1, device_id=toward(way), device_id_type=MESH)
+    own[2].start()
     for n in range(tiles):
         w_cp[n].start()
-    own[2].start()
-    own[3].start()
-    for k in range(1, nd):
+    own[3].wait()
+    for k in range(1, nd):
+        for b in range(blocks):
+            a_out[k, b] = a_own[at_owner(dp_peer(k), b)]
         a_copy(k, dp).start()
-    send_own(half, chunks)
+    for b in range(blocks):
+        a_in[dp, b] = a_own[at_owner(dp, b)]
 
     for d in range(2, nz):
         for way in (0, 1):
@@ -735,16 +752,18 @@
                             relay.at[way, d + 1], inc=1, device_id=toward(way), device_id_type=MESH
                         )
 
-    own[0].wait()
     for k in range(1, nd):
         b_copy(k, dp_from(k)).wait_recv()
     for b in range(blocks):
-        b_sel[b] = b_all[tab[dp, b]]
+        b_sel[b] = b_from[lax.div(tab[dp, b], held), b]
     b_in[z] = b_sel[z]
     for k in range(1, nz):
         bs_copy(k, z, z_peer(k)).start()
 
     event(0)
+    advance(3)
+    event(1)
+    advance(4)
 
     own[1].wait()
     row_copy(sib).wait_recv()
@@ -756,7 +775,7 @@
     lo_part[c] = low
     lo_pair(c).start()
 
-    event(1)
+    event(2)
 
     lo_pair(1 - c).wait_recv()
     lanes = lax.broadcasted_iota(jnp.int32, (rank, block), 1)
@@ -764,20 +783,14 @@
     lo_all[z] = (low * (lanes < live[dp, z]).astype(F32)).astype(BF16)
     for k in range(1, nz):
         lo_copy(k, z).start()
-
-    event(2)
-
-    own[3].wait()
-    for k in range(1, nd):
-        a_copy(k, dp_from(k)).wait_recv()
+    advance(5)
+
+    event(3)
+    advance(6)
+    event(4)
+    advance(7)
+
     own[2].wait()
-    for b in range(blocks):
-        a_sel[b] = a_all[tab[dp, b]]
-        value = dot_nt(a_sel[b], h_v[b * block : (b + 1) * block, :])
-        for i in range(rank // piece):
-            at = b * (rank // piece) + i
-            li_part[at // nz, at % nz] = value[i * piece : (i + 1) * piece, :]
-    li_pair(c).start()
     for k in range(1, nz):
         lo_copy(k, z_from(k)).wait_recv()
     for b in range(blocks):
@@ -788,13 +801,15 @@
     for k in range(1, nd):
         ga_copy(k, dp).start()
 
-    event(3)
-
-    li_pair(1 - c).wait_recv()
-    li_sum[...] = li_part[c] + li_sib[...]
-    li_rs[z] = li_sum[z]
-    for k in range(1, nz):
-        rs_copy(k, z, z_peer(k)).start()
+    for k in range(1, nd):
+        a_copy(k, dp_from(k)).wait_recv()
+    for b in range(blocks):
+        a_sel[b] = a_in[lax.div(tab[dp, b], held), b]
+        value = dot_nt(a_sel[b], h_v[b * block : (b + 1) * block, :])
+        for i in range(rank // piece):
+            at = b * (rank // piece) + i
+            li_part[at // nz, at % nz] = value[i * piece : (i + 1) * piece, :]
+    li_pair(c).start()
 
     def keep_of(b):
         return (lax.broadcasted_iota(jnp.int32, (block, 1), 0) < live[dp, b]).astype(F32)
@@ -816,8 +831,21 @@
             return carry
         lax.fori_loop(lo, hi, one, 0)
 
-    near_tiles(0, tiles // 3)
-    event(chunks)
+    near_tiles(0, 1)
+    event(5)
+
+    li_pair(1 - c).wait_recv()
+    li_sum[...] = li_part[c] + li_sib[...]
+    li_rs[z] = li_sum[z]
+    for k in range(1, nz):
+        rs_copy(k, z, z_peer(k)).start()
+    advance(8)
+
+    near_tiles(1, 3)
+    event(6)
+    advance(9)
+    near_tiles(3, 5)
+    event(7)
 
     for k in range(1, nz):
         rs_copy(k, z_from(k), z).wait_recv()
@@ -830,16 +858,8 @@
     li_all[whole] = (total * (lanes < filled).astype(F32)).astype(BF16)
     for k in range(1, nz):
         ag_copy(k, z).start()
-
-    near_tiles(tiles // 3, 2 * tiles // 3)
-    event(chunks + 1)
-    for k in range(1, nz):
-        ag_copy(k, z_from(k)).wait_recv()
-    ag_pair(c).start()
-    near_tiles(2 * tiles // 3, tiles)
-    event(chunks + 2)
-
-    ag_pair(1 - c).wait_recv()
+    advance(10)
+    near_tiles(5, tiles)
 
     def gb_block(b):
         group = rank // piece
@@ -849,9 +869,6 @@
         gb[dp, slab(b, rank), :] = (
             adapter_scale * dot_nn(rows_of, g_all[slab(b, block), slab(j, feat)])
         ).astype(BF16)
-
-    for s in range(2):
-        gb_block(near * 2 + s)
 
     def chooser(g):
         r = lax.broadcasted_iota(jnp.int32, (held * rank, blocks * rank), 0)
@@ -870,12 +887,7 @@
             total = total + dot_nn(chooser(g), ref[g])
         return total
 
-    for k in range(1, nd):
-        ga_copy(k, dp_from(k)).wait_recv()
-    oa_v[...] = owned(ga).reshape(held, rank, ff)
-
-    for n in range(chunks + 3, 2 * chunks):
-        event(n)
+
     for s in range(2):
         b = far * 2 + s
         acc[s * block : (s + 1) * block, :] = adapter_scale * dot_nn(lo_t[b], a_sel[b])
@@ -883,27 +895,21 @@
     def drain(d):
         for way in (0, 1):
             for i in range(chunks):
-                if d < nz - 1:
-                    @pl.when(has(way, d) & has(1 - way, 1))
-                    def _():
-                        nb_copy(way, d, i).wait_send()
                 if d:
                     @pl.when(has(way, d))
                     def _():
                         sib_copy(way, d, i, c).wait_send()
 
     row_copy(j).wait_send()
-    drain(0)
     drain(1)
     for k in range(1, nd):
-        for copy in (b_copy, a_copy, ga_copy):
+        for copy in (b_copy, a_copy):
             copy(k, dp).wait_send()
     for k in range(1, nz):
         bs_copy(k, z, z_peer(k)).wait_send()
         lo_copy(k, z).wait_send()
         rs_copy(k, z, z_peer(k)).wait_send()
-        ag_copy(k, z).wait_send()
-    for copy in (lo_pair, li_pair, ag_pair):
+    for copy in (lo_pair, li_pair):
         copy(c).wait_send()
     for n in range(chunks, 2 * chunks):
         landed(n)
@@ -923,11 +929,19 @@
 
     for i in range(chunks):
         event(2 * chunks + i)
+        advance(2 * chunks + i + 3)
         landed(2 * chunks + i)
         far_chunk(i, i == chunks - 1)
         if i == 0:
-            for s in range(2):
-                gb_block(far * 2 + s)
+            for k in range(1, nz):
+                ag_copy(k, z_from(k)).wait_recv()
+            ag_pair(c).start()
+            for k in range(1, nd):
+                ga_copy(k, dp_from(k)).wait_recv()
+            oa_v[...] = owned(ga).reshape(held, rank, ff)
+            ag_pair(1 - c).wait_recv()
+            for b in range(blocks):
+                gb_block(b)
             for k in range(1, nd):
                 gb_copy(k, dp).start()
         if i == chunks - 2:
@@ -936,6 +950,10 @@
             ob_v[...] = owned(gb).reshape(held, rank, feat)
             for k in range(1, nd):
                 gb_copy(k, dp).wait_send()
+                ga_copy(k, dp).wait_send()
+            for k in range(1, nz):
+                ag_copy(k, z).wait_send()
+            ag_pair(c).wait_send()
             drain(2)
     for d in range(3, nz):
         drain(d)
@@ -969,7 +987,9 @@
     dma = lambda *s: pltpu.SemaphoreType.DMA(s)
     scratch = [
         V((group_rows, width), BF16), V((group_rows, ff), BF16), V((ff, width), BF16),
-        V((nd * held, rank, ff), BF16), V((nd * held, rank, feat), BF16),
+        V((held, rank, ff), BF16), V((held, rank, feat), BF16),
+        V((nd, blocks, rank, ff), BF16), V((nd, blocks, rank, feat), BF16),
+        V((nd, blocks, rank, ff), BF16), V((nd, blocks, rank, feat), BF16),
         V((blocks, rank, ff), BF16), V((blocks, rank, feat), BF16), V((nz, rank, feat), BF16),
         V((2, rank, block), F32), V((blocks, rank, block), BF16), V((blocks, block, rank), BF16),
         V((2, nz, piece, block), F32), V((nz, piece, block), F32), V((nz, piece, block), F32),

time: 54.6 us -> 49.7 us (0.910)
  Pallas kernels: 53.3 us -> 48.8 us
    pallas_call x1, Pallas kernels: 51.8 us -> 47.2 us  [line_shards(): pl.pallas_call(functools.partial(line_kernel, nd, nz, blocks, block, rank...]
where the time goes in v2:
time: 49.7 us; the launch traced here: 49.4 us
  Pallas kernels  48.8 us (98%)
  between operations  0.64 us (1%)
    pallas_call x1, Pallas kernels, line_shards(): pl.pallas_call(functools.partial(line_kernel, nd, nz, blocks, block, rank...  47.2 us
    pallas_call x1, Pallas kernels, line_shards(): pl.pallas_call(functools.partial(store_kernel, blocks), out_shape=tuple((...  1.56 us

profile of v2, /device:TPU:0, one launch (start us, length us, event | category | flops | bytes accessed | tf_op | source)
XLA Modules:
  0.0 49.4 jit_solution(2588139689671439081)
XLA Ops:
  0.6 47.2 %shard_map.94 = (bf16[512,1792]{1,0:T(8,128)(2,1)S(1)}, f32[6,16,1792]{2,1,0:T(8,128)S(1)}, f32[6,16,512]{2,1,0:T(8,128)S(1)}) custom-call(bf16[64,4096]{1,0:T(8,128)(2,1)} %g_ref.1, bf16[512,1792]{1,0:T(8,128)(2,1)} %h_ref.1, bf16[1792,4096]{1,0:T(8,128)(2,1)} %w_ref.1, bf16[6,16,1792]{2,1,0:T(8,128)(2,1)} %a_ref.1, bf16[6,16,512]{2,1,0:T(8,128)(2,1)} %b_ref.1, ...), custom_call_target="tpu_custom_call" | custom-call | tf_op jit(solution)/shard_map/pallas_call | solution.py:1009
  47.8 1.6 %shard_map.95 = (bf16[512,1792]{1,0:T(8,128)(2,1)}, f32[6,16,1792]{2,1,0:T(8,128)}, f32[6,16,512]{2,1,0:T(8,128)}) custom-call(bf16[512,1792]{1,0:T(8,128)(2,1)S(1)} %get-tuple-element.6.hg, f32[6,16,1792]{2,1,0:T(8,128)S(1)} %get-tuple-element.7.oa, f32[6,16,512]{2,1,0:T(8,128)S(1)} %get-tuple-element.8.ob), custom_call_target="tpu_custom_call" | custom-call | tf_op jit(solution)/shard_map/pallas_call | solution.py:1023

commit v3 on v2

--- a/solution.py
+++ b/solution.py
@@ -514,12 +514,16 @@
     )(*results)
 
 
+def far_start(z, nz, start, size, width):
+    return jnp.where(z < nz // 2, start, width - start - size)
+
+
 def line_kernel(
     nd, nz, blocks, block, rank, held, rows, sizes, ff, feat, width,
     g_ref, h_ref, w_ref, a_ref, b_ref, tab, live,
-    hg_v, oa_v, ob_v,
-    g_all, h_v, w_v, a_own, b_own, a_out, b_out, a_in, b_from, a_sel, b_sel, b_in,
-    lo_part, lo_all, lo_t, li_part, li_sib, li_sum, li_rs, li_all, ga, gb, acc,
+    hg_v, oa_v, ob_v, g_all, w_v, acc, keep_v,
+    h_v, a_own, b_own, a_out, b_out, a_in, b_from, a_sel, b_sel, b_in,
+    lo_part, lo_all, lo_t, li_part, li_sib, li_sum, li_rs, li_all, ga, gb,
     w_sem, own_sem, relay,
     nb_s, nb_r, sib_s, sib_r, row_s, row_r, bdp_s, bdp_r, adp_s, adp_r,
     bs_s, bs_r, lo_s, lo_r, rs_s, rs_r, ag_s, ag_r, pair_s, pair_r,
@@ -788,9 +792,17 @@
     event(3)
     advance(6)
     event(4)
-    advance(7)
-
+
+    for k in range(1, nd):
+        a_copy(k, dp_from(k)).wait_recv()
     own[2].wait()
+    for b in range(blocks):
+        a_sel[b] = a_in[lax.div(tab[dp, b], held), b]
+        value = dot_nt(a_sel[b], h_v[b * block : (b + 1) * block, :])
+        for i in range(rank // piece):
+            at = b * (rank // piece) + i
+            li_part[at // nz, at % nz] = value[i * piece : (i + 1) * piece, :]
+    li_pair(c).start()
     for k in range(1, nz):
         lo_copy(k, z_from(k)).wait_recv()
     for b in range(blocks):
@@ -800,16 +812,12 @@
         ).astype(BF16)
     for k in range(1, nd):
         ga_copy(k, dp).start()
-
-    for k in range(1, nd):
-        a_copy(k, dp_from(k)).wait_recv()
-    for b in range(blocks):
-        a_sel[b] = a_in[lax.div(tab[dp, b], held), b]
-        value = dot_nt(a_sel[b], h_v[b * block : (b + 1) * block, :])
-        for i in range(rank // piece):
-            at = b * (rank // piece) + i
-            li_part[at // nz, at % nz] = value[i * piece : (i + 1) * piece, :]
-    li_pair(c).start()
+    li_pair(1 - c).wait_recv()
+    li_sum[...] = li_part[c] + li_sib[...]
+    li_rs[z] = li_sum[z]
+    for k in range(1, nz):
+        rs_copy(k, z, z_peer(k)).start()
+    advance(7)
 
     def keep_of(b):
         return (lax.broadcasted_iota(jnp.int32, (block, 1), 0) < live[dp, b]).astype(F32)
@@ -827,25 +835,16 @@
                 b = near * 2 + s
                 extra = dot_nn(lo_t[b], a_sel[b, :, cols])
                 total = value[s * block : (s + 1) * block] + adapter_scale * extra
-                hg_v[slab(b, block), cols] = (total * keep_of(b)).astype(BF16)
+                hg_v[s * block : (s + 1) * block, cols] = (total * keep_of(b)).astype(BF16)
             return carry
         lax.fori_loop(lo, hi, one, 0)
 
     near_tiles(0, 1)
     event(5)
-
-    li_pair(1 - c).wait_recv()
-    li_sum[...] = li_part[c] + li_sib[...]
-    li_rs[z] = li_sum[z]
-    for k in range(1, nz):
-        rs_copy(k, z, z_peer(k)).start()
     advance(8)
-
     near_tiles(1, 3)
     event(6)
-    advance(9)
-    near_tiles(3, 5)
-    event(7)
+    near_tiles(3, 4)
 
     for k in range(1, nz):
         rs_copy(k, z_from(k), z).wait_recv()
@@ -858,6 +857,10 @@
     li_all[whole] = (total * (lanes < filled).astype(F32)).astype(BF16)
     for k in range(1, nz):
         ag_copy(k, z).start()
+    advance(9)
+
+    near_tiles(4, 5)
+    event(7)
     advance(10)
     near_tiles(5, tiles)
 
@@ -891,10 +894,11 @@
     for s in range(2):
         b = far * 2 + s
         acc[s * block : (s + 1) * block, :] = adapter_scale * dot_nn(lo_t[b], a_sel[b])
-
-    def drain(d):
+        keep_v[s * block : (s + 1) * block, :] = jnp.broadcast_to(keep_of(b), (block, 128))
+
+    def drain(d, stop=chunks, first=0):
         for way in (0, 1):
-            for i in range(chunks):
+            for i in range(first, stop):
                 if d:
                     @pl.when(has(way, d))
                     def _():
@@ -914,36 +918,33 @@
     for n in range(chunks, 2 * chunks):
         landed(n)
 
-    def far_chunk(i, last):
-        start = jnp.where(z < nz // 2, starts[i], width - starts[i] - sizes[i])
+    def far_chunk(i):
+        start = far_start(z, nz, starts[i], sizes[i], width)
         deep = pl.ds(pl.multiple_of(start, 128), sizes[i])
-        keep = jnp.concatenate([keep_of(far * 2 + s) for s in range(2)], axis=0) if last else None
-        rows_at = slab(far, pair_rows)
         for n in range(tiles):
             cols = pl.ds(n * tile, tile)
-            value = acc[:, cols] + dot_nt(g_all[rows_at, deep], w_v[cols, deep])
-            if last:
-                hg_v[rows_at, cols] = (value * keep).astype(BF16)
-            else:
-                acc[:, cols] = value
+            acc[:, cols] += dot_nt(g_all[slab(far, pair_rows), deep], w_v[cols, deep])
 
     for i in range(chunks):
         event(2 * chunks + i)
         advance(2 * chunks + i + 3)
         landed(2 * chunks + i)
-        far_chunk(i, i == chunks - 1)
         if i == 0:
             for k in range(1, nz):
                 ag_copy(k, z_from(k)).wait_recv()
             ag_pair(c).start()
-            for k in range(1, nd):
-                ga_copy(k, dp_from(k)).wait_recv()
-            oa_v[...] = owned(ga).reshape(held, rank, ff)
+        if i < chunks - 1:
+            far_chunk(i)
+        if i == 0:
             ag_pair(1 - c).wait_recv()
             for b in range(blocks):
                 gb_block(b)
             for k in range(1, nd):
                 gb_copy(k, dp).start()
+        if i == 1:
+            for k in range(1, nd):
+                ga_copy(k, dp_from(k)).wait_recv()
+            oa_v[...] = owned(ga).reshape(held, rank, ff)
         if i == chunks - 2:
             for k in range(1, nd):
                 gb_copy(k, dp_from(k)).wait_recv()
@@ -955,18 +956,37 @@
                 ag_copy(k, z).wait_send()
             ag_pair(c).wait_send()
             drain(2)
+            for d in range(3, nz):
+                drain(d, chunks - 1)
     for d in range(3, nz):
-        drain(d)
-
-
-def store_kernel(blocks, hg, oa, ob, hg_out, oa_out, ob_out, sem):
-    size = hg.shape[0] // blocks
-    copies = [
-        (hg.at[pl.ds(b * size, size)], hg_out.at[pl.ds(b * size, size)]) for b in range(blocks)
-    ] + [(oa, oa_out), (ob, ob_out)]
+        drain(d, chunks, chunks - 1)
+
+
+def last_kernel(
+    nz, size, hg, oa, ob, g_all, w_v, acc, keep_v, hg_out, oa_out, ob_out, far_v, sem, tile_sem
+):
+    z = lax.div(lax.axis_index("seqtp"), 2)
+    near = lax.div(z, 2)
+    pair_rows, ff = hg.shape
+    width = w_v.shape[1]
+    tile = 256
+    near_rows = pl.ds(pl.multiple_of(near * pair_rows, pair_rows), pair_rows)
+    far_rows = pl.ds(pl.multiple_of((1 - near) * pair_rows, pair_rows), pair_rows)
+    copies = [(hg, hg_out.at[near_rows]), (oa, oa_out), (ob, ob_out)]
     copies = [pltpu.make_async_copy(s, o, sem.at[i]) for i, (s, o) in enumerate(copies)]
     for copy in copies:
         copy.start()
+    start = far_start(z, nz, width - size, size, width)
+    deep = pl.ds(pl.multiple_of(start, 128), size)
+    keep = keep_v[:, :1]
+    for n in range(ff // tile):
+        cols = pl.ds(n * tile, tile)
+        value = acc[:, cols] + dot_nt(g_all[far_rows, deep], w_v[cols, deep])
+        far_v[:, cols] = (value * keep).astype(BF16)
+        copies.append(
+            pltpu.make_async_copy(far_v.at[:, cols], hg_out.at[far_rows, cols], tile_sem.at[n])
+        )
+        copies[-1].start()
     for copy in copies:
         copy.wait()
 
@@ -986,8 +1006,7 @@
     V = pltpu.VMEM
     dma = lambda *s: pltpu.SemaphoreType.DMA(s)
     scratch = [
-        V((group_rows, width), BF16), V((group_rows, ff), BF16), V((ff, width), BF16),
-        V((held, rank, ff), BF16), V((held, rank, feat), BF16),
+        V((group_rows, ff), BF16), V((held, rank, ff), BF16), V((held, rank, feat), BF16),
         V((nd, blocks, rank, ff), BF16), V((nd, blocks, rank, feat), BF16),
         V((nd, blocks, rank, ff), BF16), V((nd, blocks, rank, feat), BF16),
         V((blocks, rank, ff), BF16), V((blocks, rank, feat), BF16), V((nz, rank, feat), BF16),
@@ -995,7 +1014,6 @@
         V((2, nz, piece, block), F32), V((nz, piece, block), F32), V((nz, piece, block), F32),
         V((nz, piece, block), F32), V((ntp, piece, block), BF16),
         V((nd, blocks * rank, ff), BF16), V((nd, blocks * rank, feat), BF16),
-        V((2 * block, ff), F32),
         dma(tiles), dma(4), pltpu.SemaphoreType.REGULAR((2, nz)),
         dma(2, nz, chunks), dma(2, nz + 1, chunks), dma(2, nz, chunks), dma(2, nz, chunks),
         pltpu.SemaphoreType.DMA, pltpu.SemaphoreType.DMA,
@@ -1011,21 +1029,27 @@
             line_kernel, nd, nz, blocks, block, rank, held, rows, sizes, ff, feat, width
         ),
         out_shape=(
-            V((group_rows, ff), BF16), V((held, rank, ff), F32), V((held, rank, feat), F32),
+            V((2 * block, ff), BF16), V((held, rank, ff), F32), V((held, rank, feat), F32),
+            V((group_rows, width), BF16), V((ff, width), BF16), V((2 * block, ff), F32),
+            V((2 * block, 128), F32),
         ),
         in_specs=[hbm] * 5 + [smem] * 2,
-        out_specs=(vmem,) * 3,
+        out_specs=(vmem,) * 7,
         scratch_shapes=scratch,
         compiler_params=pltpu.CompilerParams(
-            collective_id=1, has_side_effects=True, vmem_limit_bytes=61 * 1024 * 1024
+            collective_id=1, has_side_effects=True, vmem_limit_bytes=41 * 1024 * 1024
         ),
     )(g, h, w, a, bm, tab, live)
     return pl.pallas_call(
-        functools.partial(store_kernel, blocks),
-        out_shape=tuple(jax.ShapeDtypeStruct(x.shape, x.dtype) for x in results),
-        in_specs=[vmem] * 3,
+        functools.partial(last_kernel, nz, sizes[-1]),
+        out_shape=(
+            jax.ShapeDtypeStruct((group_rows, ff), BF16),
+            jax.ShapeDtypeStruct((held, rank, ff), F32),
+            jax.ShapeDtypeStruct((held, rank, feat), F32),
+        ),
+        in_specs=[vmem] * 7,
         out_specs=(hbm,) * 3,
-        scratch_shapes=[dma(blocks + 2)],
+        scratch_shapes=[V((2 * block, ff), BF16), dma(3), dma(tiles)],
         compiler_params=pltpu.CompilerParams(vmem_limit_bytes=8 * 1024 * 1024),
     )(*results)
 

time: 49.7 us -> 48.5 us (0.976)
  Pallas kernels: 48.8 us -> 47.6 us
    pallas_call x1, Pallas kernels: 47.2 us -> 45.6 us  [line_shards(): pl.pallas_call(functools.partial(line_kernel, nd, nz, blocks, block, rank...]
where the time goes in v3:
time: 48.5 us; the launch traced here: 48.3 us
  Pallas kernels  47.6 us (98%)
  between operations  0.64 us (1%)
    pallas_call x1, Pallas kernels, line_shards(): pl.pallas_call(functools.partial(line_kernel, nd, nz, blocks, block, rank...  45.6 us
    pallas_call x1, Pallas kernels, line_shards(): pl.pallas_call(functools.partial(last_kernel, nz, sizes[-1]), out_shape=(...  2.06 us

profile of v3, /device:TPU:0, one launch (start us, length us, event | category | flops | bytes accessed | tf_op | source)
XLA Modules:
  0.0 48.3 jit_solution(12647732909112540567)
XLA Ops:
  0.6 45.6 %shard_map.94 = (bf16[256,1792]{1,0:T(8,128)(2,1)S(1)}, f32[6,16,1792]{2,1,0:T(8,128)S(1)}, f32[6,16,512]{2,1,0:T(8,128)S(1)}, bf16[512,4096]{1,0:T(8,128)(2,1)S...) custom-call(bf16[64,4096]{1,0:T(8,128)(2,1)} %g_ref.1, ...), custom_call_target="tpu_custom_call" | custom-call | tf_op jit(solution)/shard_map/pallas_call | solution.py:1027
  46.2 2.1 %shard_map.95 = (bf16[512,1792]{1,0:T(8,128)(2,1)}, f32[6,16,1792]{2,1,0:T(8,128)}, f32[6,16,512]{2,1,0:T(8,128)}) custom-call(bf16[256,1792]{1,0:T(8,128)(2,1)S(1)} %get-tuple-element.10.hg, f32[6,16,1792]{2,1,0:T(8,128)S(1)} %get-tuple-element.11.oa, f32[6,16,512]{2,1,0:T(8,128)S(1)} %get-tuple-element.12.ob, ...), custom_call_target="tpu_custom_call" | custom-call | tf_op jit(solution)/shard_map/pallas_call | solution.py:1043

commit v4 on v3

--- a/solution.py
+++ b/solution.py
@@ -769,6 +769,7 @@
     event(1)
     advance(4)
 
+    event(2)
     own[1].wait()
     row_copy(sib).wait_recv()
     for k in range(1, nz):
@@ -779,8 +780,6 @@
     lo_part[c] = low
     lo_pair(c).start()
 
-    event(2)
-
     lo_pair(1 - c).wait_recv()
     lanes = lax.broadcasted_iota(jnp.int32, (rank, block), 1)
     low = lo_part[0] + lo_part[1]
@@ -803,6 +802,12 @@
             at = b * (rank // piece) + i
             li_part[at // nz, at % nz] = value[i * piece : (i + 1) * piece, :]
     li_pair(c).start()
+    li_pair(1 - c).wait_recv()
+    li_sum[...] = li_part[c] + li_sib[...]
+    li_rs[z] = li_sum[z]
+    for k in range(1, nz):
+        rs_copy(k, z, z_peer(k)).start()
+    advance(7)
     for k in range(1, nz):
         lo_copy(k, z_from(k)).wait_recv()
     for b in range(blocks):
@@ -812,12 +817,6 @@
         ).astype(BF16)
     for k in range(1, nd):
         ga_copy(k, dp).start()
-    li_pair(1 - c).wait_recv()
-    li_sum[...] = li_part[c] + li_sib[...]
-    li_rs[z] = li_sum[z]
-    for k in range(1, nz):
-        rs_copy(k, z, z_peer(k)).start()
-    advance(7)
 
     def keep_of(b):
         return (lax.broadcasted_iota(jnp.int32, (block, 1), 0) < live[dp, b]).astype(F32)
@@ -858,10 +857,11 @@
     for k in range(1, nz):
         ag_copy(k, z).start()
     advance(9)
+    advance(10)
 
     near_tiles(4, 5)
     event(7)
-    advance(10)
+    advance(11)
     near_tiles(5, tiles)
 
     def gb_block(b):
@@ -927,7 +927,6 @@
 
     for i in range(chunks):
         event(2 * chunks + i)
-        advance(2 * chunks + i + 3)
         landed(2 * chunks + i)
         if i == 0:
             for k in range(1, nz):

time: 48.5 us -> 48.5 us (level)
  no operation moved by 1% of the time
where the time goes in v4:
time: 48.5 us; the launch traced here: 48.3 us
  Pallas kernels  47.7 us (98%)
  between operations  0.64 us (1%)
    pallas_call x1, Pallas kernels, line_shards(): pl.pallas_call(functools.partial(line_kernel, nd, nz, blocks, block, rank...  45.6 us
    pallas_call x1, Pallas kernels, line_shards(): pl.pallas_call(functools.partial(last_kernel, nz, sizes[-1]), out_shape=(...  2.07 us

profile of v4, /device:TPU:0, one launch (start us, length us, event | category | flops | bytes accessed | tf_op | source)
XLA Modules:
  0.0 48.3 jit_solution(956318726883852044)
XLA Ops:
  0.6 45.6 %shard_map.94 = (bf16[256,1792]{1,0:T(8,128)(2,1)S(1)}, f32[6,16,1792]{2,1,0:T(8,128)S(1)}, f32[6,16,512]{2,1,0:T(8,128)S(1)}, bf16[512,4096]{1,0:T(8,128)(2,1)S...) custom-call(bf16[64,4096]{1,0:T(8,128)(2,1)} %g_ref.1, ...), custom_call_target="tpu_custom_call" | custom-call | tf_op jit(solution)/shard_map/pallas_call | solution.py:1026
  46.2 2.1 %shard_map.95 = (bf16[512,1792]{1,0:T(8,128)(2,1)}, f32[6,16,1792]{2,1,0:T(8,128)}, f32[6,16,512]{2,1,0:T(8,128)}) custom-call(bf16[256,1792]{1,0:T(8,128)(2,1)S(1)} %get-tuple-element.10.hg, f32[6,16,1792]{2,1,0:T(8,128)S(1)} %get-tuple-element.11.oa, f32[6,16,512]{2,1,0:T(8,128)S(1)} %get-tuple-element.12.ob, ...), custom_call_target="tpu_custom_call" | custom-call | tf_op jit(solution)/shard_map/pallas_call | solution.py:1042
